TPU v7x, 512 devices: a whole 4x8x8 slice. The times are simulated.
512 devices in a mesh: vocab: 64 (over x, y, core), tok: 8 (over z).
Axes of the slice: x: 4, y: 8, z: 8, core: 2. Of those that a mesh axis runs over, the one named last changes fastest.
Arguments:
- hidden: bfloat16 [1024, 3584], P('tok'), may hold values from -320 to 320
- head: bfloat16 [3584, 98304], P('tok', 'vocab'), may hold values from -2 to 2
- teacher: bfloat16 [1024, 98304], P('tok', 'vocab'), may hold values from 0 to 1, as said below
- block_ids: int32 [8, 16], P('tok'), may hold values from -1 to 191, as said below
- counts: int32 [8], P('tok'), may hold values from 8 to 16
Outputs:
- lse: float32 [1024], P('tok')
- kl: float32 [1024], P('tok')
- grad_hidden: float32 [1024, 3584], P('tok', 'vocab')
- grad_head: bfloat16 [3584, 98304], P('tok', 'vocab')
Inputs may be any that keep to these rules, and one draw needn't show every extreme that they name: `block_ids`: row b lists counts[b] distinct teacher blocks (block k covers columns 512 * k to 512 * k + 511) in its first counts[b] entries; the rest of the row is -1. `teacher`: every entry is positive.
All inputs are finite; a program needn't handle non-finite values.
Results may differ from a plain program's by a relative error of at most 0.0055.
Values may be sent and summed in bfloat16 or wider, within the bound.
A program may use at most 64 MiB of HBM per device.

v0:
```python
import jax
import jax.numpy as jnp
from jax import lax
from jax.sharding import PartitionSpec as P

BLK = 512
loss_scale = 1024.0


def local_stats(logits, teacher, listed):
    teacher_f = teacher.astype(jnp.float32)
    kept = jnp.where(listed, teacher_f, 0.0)
    local_top = jnp.max(logits, axis=1)
    local_sum = jnp.sum(jnp.exp(logits - local_top[:, None]), axis=1)
    local_mass = jnp.sum(kept, axis=1)
    local_part = jnp.sum(jnp.where(listed, teacher_f * (jnp.log(teacher_f) - logits), 0.0), axis=1)
    return (kept, (local_top, local_sum, local_mass, local_part))


def finish_stats(logits, kept, global_top, total_sum, total_mass, total_part):
    lse = global_top + jnp.log(total_sum)
    kl = total_part / total_mass - jnp.log(total_mass) + lse
    student = jnp.exp(logits - lse[:, None])
    delta = (loss_scale * (student - kept / total_mass[:, None])).astype(jnp.bfloat16)
    return (lse, kl, delta)


def listed_columns(block_ids, counts, column_block, token_count):
    live_slot = jnp.arange(block_ids.shape[1], dtype=jnp.int32)[None, :] < counts[:, None]
    block_hit = jnp.any(
        (block_ids[:, :, None] == column_block[None, None, :]) & live_slot[:, :, None], axis=1
    )
    token_blocks = block_hit.shape[0]
    width = column_block.shape[0]
    return jnp.broadcast_to(
        block_hit[:, None, :], (token_blocks, token_count // token_blocks, width)
    ).reshape(token_count, width)


def per_device(hidden, head, teacher, block_ids, counts):
    token_count = hidden.shape[0]
    column_count = head.shape[1]
    full_head = lax.all_gather(head, "tok", axis=0, tiled=True)
    logits = jnp.dot(hidden, full_head, preferred_element_type=jnp.float32)
    first_column = lax.axis_index("vocab") * column_count
    column_block = (first_column + jnp.arange(column_count, dtype=jnp.int32)) // BLK
    listed = listed_columns(block_ids, counts, column_block, token_count)
    kept, stats_here = local_stats(logits, teacher, listed)
    local_top, local_sum, local_mass, local_part = stats_here
    global_top = lax.pmax(local_top, "vocab")
    scaled_sum = local_sum * jnp.exp(local_top - global_top)
    total_sum, total_mass, total_part = lax.psum((scaled_sum, local_mass, local_part), "vocab")
    lse, kl, delta = finish_stats(logits, kept, global_top, total_sum, total_mass, total_part)
    grad_hidden = lax.psum_scatter(
        lax.dot_general(
            full_head, delta, (((1,), (1,)), ((), ())), preferred_element_type=jnp.float32
        ),
        "vocab",
        scatter_dimension=0,
        tiled=True,
    ).T
    slices = lax.all_to_all(hidden, "tok", split_axis=1, concat_axis=0, tiled=True)
    grad_head = lax.dot_general(
        slices,
        lax.all_gather(delta, "tok", axis=0, tiled=True),
        (((0,), (0,)), ((), ())),
        preferred_element_type=jnp.float32,
    ).astype(jnp.bfloat16)
    return (lse, kl, grad_hidden, grad_head)


def solution(mesh):
    placed = (P("tok", None), P("tok", "vocab"), P("tok", "vocab"), P("tok", None), P("tok"))
    return jax.shard_map(
        per_device,
        mesh=mesh,
        in_specs=placed,
        out_specs=(P("tok"), P("tok"), P("tok", "vocab"), P("tok", "vocab")),
        check_vma=False,
    )
```

profile of v0, /device:TPU:1, one launch (start us, length us, event | category | flops | bytes accessed | tf_op | source)
XLA Modules:
  0.0 657.2 jit_solution(4507832720757288670)
XLA Ops:
  7.2 0.0 all-gather.3.cloned.1.call-start
  7.2 0.7 all-gather.3.cloned.1.call-update
  7.9 0.0 all-reduce.4.cloned.1.call-start
  8.6 0.8 and_reduce_fusion
  9.4 0.0 copy-start.2
  9.4 128.1 %all-gather.3.cloned.1.call-done = bf16[3584,1536]{1,0:T(8,128)(2,1)} async-done(((bf16[448,1536]{1,0:T(8,128)(2,1)}), bf16[3584,1536]{1,0:T(8,128)(2,1)}) %all-gather.3.cloned.1.call-update) | async-done | bytes 11010064 | tf_op jit(solution)/shard_map/all_gather | solution.py:43
  137.5 6.1 fusion.14
  143.6 124.3 %pmax.7 = f32[128]{0:T(128)S(1)} all-reduce(f32[128]{0:T(128)S(1)} %get-tuple-element.28), channel_id=1, replica_groups=mesh['vocab'=64,'tok'=8] {'vocab'}, use_global_device_ids=true, to_apply=%region_1.2 | all-reduce | flops 128 | bytes 1024 | tf_op jit(solution)/shard_map/pmax | solution.py:50
  267.8 0.0 copy-done.2
  267.8 0.5 fusion.9
  268.3 128.3 %all-reduce.1 = (f32[128]{0:T(128)S(1)}, f32[128]{0:T(128)S(1)}, f32[128]{0:T(128)S(1)}) all-reduce(f32[128]{0:T(128)S(1)} %exponential_multiply_fusion, f32[128]{0:T(128)S(1)} %get-tuple-element.22, f32[128]{0:T(128)S(1)} %get-tuple-element.20), channel_id=1, replica_groups=mesh['vocab'=64,'tok'=8] {'vocab'}, use_global_device_ids=true, to_apply=%region_3.4 | all-reduce | flops 384 | bytes 3072 | tf_op jit(solution)/shard_map/psum | solution.py:52
  396.6 0.5 subtract_add_fusion
  397.1 0.0 copy-start.3
  397.1 0.3 fusion.10
  397.4 0.0 copy-start.1
  397.4 0.0 copy-start
  397.4 9.1 %convolution_bitcast_fusion = f32[3584,128]{0,1:T(8,128)} fusion(bf16[128,1536]{1,0:T(8,128)(2,1)S(1)} %fusion.10, bf16[3584,1536]{1,0:T(8,128)(2,1)} %all-gather.3.cloned.1.call-done), kind=kOutput, calls=%fused_computation | convolution fusion | flops 1409286144 | bytes 13238272 | tf_op jit(solution)/shard_map/dot_general | solution.py:55
  406.6 0.0 copy-done.3
  406.6 0.0 copy-done.1
  406.6 0.0 all-reduce.4.cloned.1.call-update
  406.6 0.0 all-gather.5.cloned.1.call-start
  406.6 0.7 all-gather.5.cloned.1.call-update
  407.3 0.0 copy-done
  407.3 1.3 copy.16
  408.6 3.8 all-to-all-start
  412.4 1.3 dynamic-slice
  414.3 182.0 %all-reduce.4.cloned.1.call-done = f32[3584,128]{0,1:T(8,128)} async-done(((f32[3584,128]{0,1:T(8,128)}), f32[3584,128]{0,1:T(8,128)}) %all-reduce.4.cloned.1.call-update) | async-done | bytes 1835024
  596.3 1.0 dynamic-slice_bitcast_fusion
  597.3 0.7 copy.18
  598.0 0.0 all-to-all-done
  598.0 48.1 %all-gather.5.cloned.1.call-done = bf16[1024,1536]{1,0:T(8,128)(2,1)} async-done(((bf16[128,1536]{1,0:T(8,128)(2,1)}), bf16[1024,1536]{1,0:T(8,128)(2,1)}) %all-gather.5.cloned.1.call-update) | async-done | bytes 3145744 | tf_op jit(solution)/shard_map/all_gather | solution.py:65
  646.1 4.6 fusion
  (3 shorter events, 0.0 us)
Async XLA Ops:
  7.2 130.3 %all-gather.3.cloned.1.call-start = ((), (), s32[]{:S(2)}) async-start(), calls=%async_computation.1 | async-start | bytes 12386304 | tf_op jit(solution)/shard_map/all_gather | solution.py:43
  7.9 588.4 %all-reduce.4.cloned.1.call-start = ((), (), s32[]{:S(2)}) async-start(), calls=%async_computation.3 | async-start | bytes 3670016
  9.4 258.5 %copy-start.2 = (bf16[128,1536]{1,0:T(8,128)(2,1)S(1)}, bf16[128,1536]{1,0:T(8,128)(2,1)}, u32[]{:S(2)}) copy-start(bf16[128,1536]{1,0:T(8,128)(2,1)} %param.7) | copy-start | bytes 1179652
  397.1 9.5 %copy-start.3 = (f32[128]{0:T(128)}, f32[128]{0:T(128)S(1)}, u32[]{:S(2)}) copy-start(f32[128]{0:T(128)S(1)} %get-tuple-element.27) | copy-start | bytes 1540
  397.4 9.2 %copy-start.1 = (bf16[128,1536]{1,0:T(8,128)(2,1)}, bf16[128,1536]{1,0:T(8,128)(2,1)S(1)}, u32[]{:S(2)}) copy-start(bf16[128,1536]{1,0:T(8,128)(2,1)S(1)} %fusion.10) | copy-start | bytes 1179652
  397.4 9.9 %copy-start = (bf16[128,3584]{1,0:T(8,128)(2,1)S(1)}, bf16[128,3584]{1,0:T(8,128)(2,1)}, u32[]{:S(2)}) copy-start(bf16[128,3584]{1,0:T(8,128)(2,1)} %param.5) | copy-start | bytes 2752516
  406.6 239.5 %all-gather.5.cloned.1.call-start = ((), (), s32[]{:S(2)}) async-start(), calls=%async_computation.2 | async-start | bytes 3538944 | tf_op jit(solution)/shard_map/all_gather | solution.py:65
  408.6 189.4 %all-to-all-start = ((bf16[128,8,448]{0,2,1:T(8,128)(2,1)}), bf16[128,8,448]{0,2,1:T(8,128)(2,1)S(1)}, u32[]{:S(2)}, u32[]{:S(2)}) async-start(bf16[128,8,448]{0,2,1:T(8,128)(2,1)} %bitcast.4), calls=%async_computation | async-start | bytes 1835008 | tf_op jit(solution)/shard_map/all_to_all | solution.py:62
Sparse Core Ops, SparseCore 0:
  10.1 127.3 all-gather.2
  406.7 189.5 all-reduce.3
  598.4 47.6 all-gather.4
where the time goes:
time: 658 us; the launch traced here: 657 us
  waiting for transfers between devices  360 us (55%)
  blocking collectives  253 us (38%)
  matrix products  19.8 us (3%)
  between operations  15.1 us (2%)
    unnamed x4, waiting for transfers between devices  183 us
    psum x1, blocking collectives, per_device(): lax.psum((scaled_sum, local_mass, local_part), 'vocab')  128 us
    all_gather x1, waiting for transfers between devices, per_device(): full_head = lax.all_gather(head, 'tok', axis=0, tiled=True)  128 us
    pmax x1, blocking collectives, per_device(): global_top = lax.pmax(local_top, 'vocab')  124 us
    all_gather x1, waiting for transfers between devices, per_device(): lax.all_gather(delta, 'tok', axis=0, tiled=True)  48.1 us
  transfers between devices with their start and end apart: 4, of which 3 were waited for; matrix products, arithmetic and copies ran while one was open for 1% of the time, Pallas kernels for 0%

commit v1 on v0

--- a/solution.py
+++ b/solution.py
@@ -62,7 +62,9 @@
     slices = lax.all_to_all(hidden, "tok", split_axis=1, concat_axis=0, tiled=True)
     grad_head = lax.dot_general(
         slices,
-        lax.all_gather(delta, "tok", axis=0, tiled=True),
+        jnp.concatenate(
+            lax.all_to_all(jnp.stack([delta] * lax.axis_size("tok")), "tok", 0, 0), axis=0
+        ),
         (((0,), (0,)), ((), ())),
         preferred_element_type=jnp.float32,
     ).astype(jnp.bfloat16)

time: 658 us -> 634 us (0.964)
  waiting for transfers between devices: 360 us -> 319 us
  starting transfers between devices: 3.94 us -> 15.4 us
    all_gather x1 -> x0, waiting for transfers between devices: 48.1 us -> none  [per_device(): lax.all_gather(delta, 'tok', axis=0, tiled=True)]
    unnamed x4 -> x3, waiting for transfers between devices: 183 us -> 193 us
    all_to_all x1, starting transfers between devices: 3.83 us -> 10.9 us  [per_device(): lax.all_to_all(hidden, 'tok', split_axis=1, concat_axis=0, tiled=True)]
  transfers between devices with their start and end apart: 4 -> 4, of which waited for: 3 -> 2; matrix products, arithmetic and copies ran while one was open for 1% -> 3% of each run, Pallas kernels for 0% -> 0%
where the time goes in v1:
time: 634 us; the launch traced here: 631 us
  waiting for transfers between devices  319 us (50%)
  blocking collectives  253 us (40%)
  matrix products  19.3 us (3%)
  starting transfers between devices  15.4 us (2%)
  between operations  15.4 us (2%)
  local copies, waits for them, and re-layouts  7.08 us (1%)
    unnamed x3, waiting for transfers between devices  193 us
    psum x1, blocking collectives, per_device(): lax.psum((scaled_sum, local_mass, local_part), 'vocab')  129 us
    all_gather x1, waiting for transfers between devices, per_device(): full_head = lax.all_gather(head, 'tok', axis=0, tiled=True)  127 us
    pmax x1, blocking collectives, per_device(): global_top = lax.pmax(local_top, 'vocab')  125 us
  transfers between devices with their start and end apart: 4, of which 2 were waited for; matrix products, arithmetic and copies ran while one was open for 3% of the time, Pallas kernels for 0%

profile of v1, /device:TPU:1, one launch (start us, length us, event | category | flops | bytes accessed | tf_op | source)
XLA Modules:
  0.0 631.2 jit_solution(16260579794564994188)
XLA Ops:
  7.2 0.0 copy-start
  7.2 0.0 copy-start.3
  7.2 0.0 all-gather.2.cloned.1.call-start
  7.2 0.7 all-gather.2.cloned.1.call-update
  7.9 2.2 copy.13
  10.1 10.9 %all-to-all-start.1 = ((bf16[128,8,448]{0,2,1:T(8,128)(2,1)}), bf16[128,8,448]{0,2,1:T(8,128)(2,1)S(1)}, u32[]{:S(2)}, u32[]{:S(2)}) async-start(bf16[128,8,448]{0,2,1:T(8,128)(2,1)} %bitcast.4), calls=%async_computation.1 | async-start | bytes 1835008 | tf_op jit(solution)/shard_map/all_to_all | solution.py:62
  21.7 0.0 copy-done.3
  21.7 0.1 and_reduce_fusion
  21.8 0.0 copy-start.1
  21.8 126.6 %all-gather.2.cloned.1.call-done = bf16[3584,1536]{1,0:T(8,128)(2,1)} async-done(((bf16[448,1536]{1,0:T(8,128)(2,1)}), bf16[3584,1536]{1,0:T(8,128)(2,1)}) %all-gather.2.cloned.1.call-update) | async-done | bytes 11010064 | tf_op jit(solution)/shard_map/all_gather | solution.py:43
  148.4 0.0 copy-done
  148.4 5.8 fusion.14
  154.2 124.7 %pmax.7 = f32[128]{0:T(128)S(1)} all-reduce(f32[128]{0:T(128)S(1)} %get-tuple-element.24), channel_id=1, replica_groups=mesh['vocab'=64,'tok'=8] {'vocab'}, use_global_device_ids=true, to_apply=%region_1.2 | all-reduce | flops 128 | bytes 1024 | tf_op jit(solution)/shard_map/pmax | solution.py:50
  278.9 0.0 copy-done.1
  278.9 0.5 fusion.9
  279.4 128.6 %all-reduce.1 = (f32[128]{0:T(128)S(1)}, f32[128]{0:T(128)S(1)}, f32[128]{0:T(128)S(1)}) all-reduce(f32[128]{0:T(128)S(1)} %exponential_multiply_fusion, f32[128]{0:T(128)S(1)} %get-tuple-element.18, f32[128]{0:T(128)S(1)} %get-tuple-element.16), channel_id=1, replica_groups=mesh['vocab'=64,'tok'=8] {'vocab'}, use_global_device_ids=true, to_apply=%region_3.4 | all-reduce | flops 384 | bytes 3072 | tf_op jit(solution)/shard_map/psum | solution.py:52
  408.0 0.5 subtract_add_fusion
  408.5 0.0 copy-start.2
  408.5 0.3 fusion.10
  408.8 0.0 all-to-all-done.1
  408.8 1.9 stack.2
  410.7 0.0 copy-done.2
  410.7 4.5 all-to-all-start
  415.1 0.0 all-reduce.4.cloned.1.call-start
  415.2 8.9 %convolution_bitcast_fusion = f32[3584,128]{0,1:T(8,128)} fusion(bf16[128,1536]{1,0:T(8,128)(2,1)S(1)} %fusion.10, bf16[3584,1536]{1,0:T(8,128)(2,1)} %all-gather.2.cloned.1.call-done), kind=kOutput, calls=%fused_computation | convolution fusion | flops 1409286144 | bytes 13238272 | tf_op jit(solution)/shard_map/dot_general | solution.py:55
  424.1 0.0 all-reduce.4.cloned.1.call-update
  424.2 1.3 dynamic-slice
  426.1 192.1 %all-reduce.4.cloned.1.call-done = f32[3584,128]{0,1:T(8,128)} async-done(((f32[3584,128]{0,1:T(8,128)}), f32[3584,128]{0,1:T(8,128)}) %all-reduce.4.cloned.1.call-update) | async-done | bytes 1835024
  618.2 1.0 dynamic-slice_bitcast_fusion
  619.1 0.7 copy.14
  619.8 0.0 all-to-all-done
  619.8 4.5 fusion.1
  (3 shorter events, 0.0 us)
Async XLA Ops:
  7.2 141.3 %copy-start = (bf16[128,3584]{1,0:T(8,128)(2,1)S(1)}, bf16[128,3584]{1,0:T(8,128)(2,1)}, u32[]{:S(2)}) copy-start(bf16[128,3584]{1,0:T(8,128)(2,1)} %param.5) | copy-start | bytes 2752516
  7.2 14.5 %copy-start.3 = (s32[1,16]{1,0:T(1,128)S(1)}, s32[1,16]{1,0:T(1,128)}, u32[]{:S(2)}) copy-start(s32[1,16]{1,0:T(1,128)} %param.8) | copy-start | bytes 196
  7.2 141.2 %all-gather.2.cloned.1.call-start = ((), (), s32[]{:S(2)}) async-start(), calls=%async_computation.2 | async-start | bytes 12386304 | tf_op jit(solution)/shard_map/all_gather | solution.py:43
  10.1 398.6 %all-to-all-start.1 = ((bf16[128,8,448]{0,2,1:T(8,128)(2,1)}), bf16[128,8,448]{0,2,1:T(8,128)(2,1)S(1)}, u32[]{:S(2)}, u32[]{:S(2)}) async-start(bf16[128,8,448]{0,2,1:T(8,128)(2,1)} %bitcast.4), calls=%async_computation.1 | async-start | bytes 1835008 | tf_op jit(solution)/shard_map/all_to_all | solution.py:62
  21.8 257.1 %copy-start.1 = (bf16[128,1536]{1,0:T(8,128)(2,1)S(1)}, bf16[128,1536]{1,0:T(8,128)(2,1)}, u32[]{:S(2)}) copy-start(bf16[128,1536]{1,0:T(8,128)(2,1)} %param.7) | copy-start | bytes 1179652
  408.5 2.2 copy-start.2
  410.7 209.2 %all-to-all-start = ((bf16[8,128,1536]{2,1,0:T(8,128)(2,1)}), bf16[8,128,1536]{2,1,0:T(8,128)(2,1)}, u32[]{:S(2)}, u32[]{:S(2)}) async-start(bf16[8,128,1536]{2,1,0:T(8,128)(2,1)} %stack.2), calls=%async_computation | async-start | bytes 6291456 | tf_op jit(solution)/shard_map/all_to_all | solution.py:66
  415.1 203.0 %all-reduce.4.cloned.1.call-start = ((), (), s32[]{:S(2)}) async-start(), calls=%async_computation.3 | async-start | bytes 3670016
Sparse Core Ops, SparseCore 0:
  10.1 138.3 all-gather.1
  424.3 193.8 all-reduce.3
